TPU v7x, 32 devices: a whole 2x2x4 slice. The times are simulated.
32 devices in a mesh: row: 8 (over z, y), feat: 4 (over x, core).
Axes of the slice: x: 2, y: 2, z: 4, core: 2. Of those that a mesh axis runs over, the one named last changes fastest.
Arguments:
- design: bfloat16 [1024, 65536], P('row', 'feat'), may hold values from -0.0234375 to 0.0234375
- targets: bfloat16 [1024, 48], P('row'), may hold values from -6 to 6
- factor: float32 [65536, 256], P(('feat', 'row')), may hold values from -0.09375 to 0.09375
- weights: float32 [256], replicated, may hold values from 0.3 to 3
- penalty: float32 [48], replicated, may hold values from 0.05 to 0.5
Outputs:
- solution: float32 [65536, 48], P(('feat', 'row'))
- residual: float32 [65536, 48], P(('feat', 'row'))
All inputs are finite; a program needn't handle non-finite values.
Results may differ from a plain program's by a relative error of at most 0.024.
Values may be sent and summed in bfloat16 or wider, within the bound.
A program may use at most 64 MiB of HBM per device.

v0:
```python
import jax
import jax.numpy as jnp
from jax import lax
from jax.sharding import PartitionSpec as P

ITERS = 3


def shards(design, targets, factor, weights, penalty):

    def normal_terms(rows_low):
        return lax.psum_scatter(
            lax.dot_general(
                design, rows_low, (((0,), (0,)), ((), ())), preferred_element_type=jnp.float32
            ),
            "row",
            scatter_dimension=0,
            tiled=True,
        )

    def precondition(residual):
        projected = jnp.dot(factor.T, residual, precision=lax.Precision.HIGHEST)
        projected = lax.psum(projected, ("row", "feat"))
        search = residual + jnp.dot(
            factor, weights[:, None] * projected, precision=lax.Precision.HIGHEST
        )
        inner = lax.psum(jnp.sum(residual * search, axis=0), ("row", "feat"))
        return (search, inner)

    residual = normal_terms(targets)
    solution = jnp.zeros_like(residual)
    search, inner = precondition(residual)
    direction = search
    for step_index in range(ITERS):
        dir_low = direction.astype(jnp.bfloat16)
        row_values = lax.psum(
            jnp.dot(
                design,
                lax.all_gather(dir_low, "row", axis=0, tiled=True),
                preferred_element_type=jnp.float32,
            ),
            "feat",
        )
        row_low = row_values.astype(jnp.bfloat16)
        dir_slice = direction
        local_part = jnp.sum(row_values * row_low.astype(jnp.float32), axis=0) / lax.axis_size(
            "feat"
        )
        local_part = local_part + penalty * jnp.sum(dir_slice * dir_slice, axis=0)
        curvature = lax.psum(local_part, ("row", "feat"))
        hessian_dir = normal_terms(row_low) + penalty[None, :] * dir_slice
        step_size = inner / curvature
        solution = solution + step_size[None, :] * dir_slice
        residual = residual - step_size[None, :] * hessian_dir
        if step_index + 1 < ITERS:
            search, inner_next = precondition(residual)
            direction = search + (inner_next / inner)[None, :] * direction
            inner = inner_next
    return (solution, residual)


def solution(mesh):
    return jax.shard_map(
        shards,
        mesh=mesh,
        in_specs=(P("row", "feat"), P("row", None), P(("feat", "row"), None), P(), P()),
        out_specs=(P(("feat", "row"), None), P(("feat", "row"), None)),
        check_vma=False,
    )
```

profile of v0, /device:TPU:0, one launch (start us, length us, event | category | flops | bytes accessed | tf_op | source)
XLA Modules:
  0.0 737.3 jit_solution(17198309492776830987)
XLA Ops:
  7.2 4.7 fusion.13
  12.0 77.5 %reduce-scatter.5.cloned.1.call-done = f32[2048,48]{0,1:T(8,128)} async-done(((f32[16384,48]{0,1:T(8,128)}), f32[2048,48]{0,1:T(8,128)}) %reduce-scatter.5.cloned.1.call-update) | async-done | bytes 393232 | tf_op jit(solution)/shard_map/reduce_scatter | solution.py:12
  89.6 4.5 convolution_bitcast_fusion.8
  94.1 40.7 %psum.84 = f32[256,48]{1,0:T(8,128)S(1)} all-reduce(f32[256,48]{1,0:T(8,128)S(1)} %convolution_bitcast_fusion.8), channel_id=1, replica_groups=mesh['row'=8,'feat'=4] {'row','feat'}, use_global_device_ids=true, to_apply=%region_1.0 | all-reduce | flops 12288 | bytes 98304 | tf_op jit(solution)/shard_map/psum | solution.py:23
  134.8 2.7 multiply_reduce_fusion.4
  137.6 43.6 %all-gather.4.cloned.1.call-done = bf16[16384,48]{0,1:T(8,128)(2,1)} async-done(((bf16[2048,48]{0,1:T(8,128)(2,1)}), bf16[16384,48]{0,1:T(8,128)(2,1)}) %all-gather.4.cloned.1.call-update) | async-done | bytes 1572880 | tf_op jit(solution)/shard_map/all_gather | solution.py:39
  181.2 4.2 convolution_bitcast_fusion.11
  185.4 10.3 %psum.86 = f32[128,48]{0,1:T(8,128)S(1)} all-reduce(f32[128,48]{0,1:T(8,128)S(1)} %convolution_bitcast_fusion.11), channel_id=1, replica_groups=mesh['row'=8,'feat'=4] {'feat'}, use_global_device_ids=true, to_apply=%region_4.0 | all-reduce | flops 6144 | bytes 49152 | tf_op jit(solution)/shard_map/psum | solution.py:36
  195.7 4.5 convolution_bitcast_fusion.2
  200.9 40.9 %all-reduce = (f32[48]{0:T(128)S(1)}, f32[48]{0:T(128)S(1)}) all-reduce(f32[48]{0:T(128)S(1)} %get-tuple-element.3, f32[48]{0:T(128)S(1)} %multiply_add_fusion.5), channel_id=1, replica_groups=mesh['row'=8,'feat'=4] {'row','feat'}, use_global_device_ids=true, to_apply=%region_3.0 | all-reduce | flops 96 | bytes 768 | tf_op jit(solution)/shard_map/psum | solution.py:27
  241.8 33.1 %reduce-scatter.7.cloned.1.call-done = f32[2048,48]{0,1:T(8,128)} async-done(((f32[16384,48]{0,1:T(8,128)}), f32[2048,48]{0,1:T(8,128)}) %reduce-scatter.7.cloned.1.call-update) | async-done | bytes 393232 | tf_op jit(solution)/shard_map/reduce_scatter | solution.py:12
  276.0 3.4 convolution_bitcast_fusion.7
  279.5 40.7 %psum.88 = f32[256,48]{1,0:T(8,128)S(1)} all-reduce(f32[256,48]{1,0:T(8,128)S(1)} %convolution_bitcast_fusion.7), channel_id=1, replica_groups=mesh['row'=8,'feat'=4] {'row','feat'}, use_global_device_ids=true, to_apply=%region_9.0 | all-reduce | flops 12288 | bytes 98304 | tf_op jit(solution)/shard_map/psum | solution.py:23
  320.2 2.8 multiply_reduce_fusion.3
  323.0 39.4 %psum.89 = f32[48]{0:T(128)S(1)} all-reduce(f32[48]{0:T(128)S(1)} %get-tuple-element.14), channel_id=1, replica_groups=mesh['row'=8,'feat'=4] {'row','feat'}, use_global_device_ids=true, to_apply=%region_11.0 | all-reduce | flops 48 | bytes 384 | tf_op jit(solution)/shard_map/psum | solution.py:27
  364.5 44.2 %all-gather.6.cloned.1.call-done = bf16[16384,48]{0,1:T(8,128)(2,1)} async-done(((bf16[2048,48]{0,1:T(8,128)(2,1)}), bf16[16384,48]{0,1:T(8,128)(2,1)}) %all-gather.6.cloned.1.call-update) | async-done | bytes 1572880 | tf_op jit(solution)/shard_map/all_gather | solution.py:39
  408.7 4.2 convolution_bitcast_fusion.10
  412.9 10.3 %psum.90 = f32[128,48]{0,1:T(8,128)S(1)} all-reduce(f32[128,48]{0,1:T(8,128)S(1)} %convolution_bitcast_fusion.10), channel_id=1, replica_groups=mesh['row'=8,'feat'=4] {'feat'}, use_global_device_ids=true, to_apply=%region_12.0 | all-reduce | flops 6144 | bytes 49152 | tf_op jit(solution)/shard_map/psum | solution.py:36
  423.2 4.5 convolution_bitcast_fusion.1
  427.9 41.2 %psum.91 = f32[48]{0:T(128)S(1)} all-reduce(f32[48]{0:T(128)S(1)} %multiply_add_fusion.4), channel_id=1, replica_groups=mesh['row'=8,'feat'=4] {'row','feat'}, use_global_device_ids=true, to_apply=%region_15.0 | all-reduce | flops 48 | bytes 384 | tf_op jit(solution)/shard_map/psum | solution.py:50
  469.1 33.4 %reduce-scatter.9.cloned.1.call-done = f32[2048,48]{0,1:T(8,128)} async-done(((f32[16384,48]{0,1:T(8,128)}), f32[2048,48]{0,1:T(8,128)}) %reduce-scatter.9.cloned.1.call-update) | async-done | bytes 393232 | tf_op jit(solution)/shard_map/reduce_scatter | solution.py:12
  503.6 3.4 convolution_bitcast_fusion.6
  507.0 40.7 %psum.92 = f32[256,48]{1,0:T(8,128)S(1)} all-reduce(f32[256,48]{1,0:T(8,128)S(1)} %convolution_bitcast_fusion.6), channel_id=1, replica_groups=mesh['row'=8,'feat'=4] {'row','feat'}, use_global_device_ids=true, to_apply=%region_17.0 | all-reduce | flops 12288 | bytes 98304 | tf_op jit(solution)/shard_map/psum | solution.py:23
  547.7 2.0 multiply_reduce_fusion.1
  549.8 39.4 %psum.93 = f32[48]{0:T(128)S(1)} all-reduce(f32[48]{0:T(128)S(1)} %get-tuple-element.16), channel_id=1, replica_groups=mesh['row'=8,'feat'=4] {'row','feat'}, use_global_device_ids=true, to_apply=%region_19.0 | all-reduce | flops 48 | bytes 384 | tf_op jit(solution)/shard_map/psum | solution.py:27
  590.2 44.2 %all-gather.8.cloned.1.call-done = bf16[16384,48]{0,1:T(8,128)(2,1)} async-done(((bf16[2048,48]{0,1:T(8,128)(2,1)}), bf16[16384,48]{0,1:T(8,128)(2,1)}) %all-gather.8.cloned.1.call-update) | async-done | bytes 1572880 | tf_op jit(solution)/shard_map/all_gather | solution.py:39
  634.4 4.2 convolution_bitcast_fusion.9
  638.6 10.3 %psum.94 = f32[128,48]{0,1:T(8,128)S(1)} all-reduce(f32[128,48]{0,1:T(8,128)S(1)} %convolution_bitcast_fusion.9), channel_id=1, replica_groups=mesh['row'=8,'feat'=4] {'feat'}, use_global_device_ids=true, to_apply=%region_20.0 | all-reduce | flops 6144 | bytes 49152 | tf_op jit(solution)/shard_map/psum | solution.py:36
  648.9 4.5 convolution_bitcast_fusion
  654.8 41.2 %psum.95 = f32[48]{0:T(128)S(1)} all-reduce(f32[48]{0:T(128)S(1)} %multiply_add_fusion.3), channel_id=1, replica_groups=mesh['row'=8,'feat'=4] {'row','feat'}, use_global_device_ids=true, to_apply=%region_23.0 | all-reduce | flops 48 | bytes 384 | tf_op jit(solution)/shard_map/psum | solution.py:50
  696.0 32.2 %reduce-scatter.11.cloned.1.call-done = f32[2048,48]{0,1:T(8,128)} async-done(((f32[16384,48]{0,1:T(8,128)}), f32[2048,48]{0,1:T(8,128)}) %reduce-scatter.11.cloned.1.call-update) | async-done | bytes 393232 | tf_op jit(solution)/shard_map/reduce_scatter | solution.py:12
  728.2 2.2 multiply_subtract_fusion
  (43 shorter events, 7.5 us)
Async XLA Ops:
  7.2 82.4 %copy-start = (f32[2048,256]{1,0:T(8,128)S(1)}, f32[2048,256]{1,0:T(8,128)}, u32[]{:S(2)}) copy-start(f32[2048,256]{1,0:T(8,128)} %param.7) | copy-start | bytes 6291460
  7.2 82.4 %reduce-scatter.5.cloned.1.call-start = ((), (), s32[]{:S(2)}) async-start(), calls=%async_computation.4 | async-start | bytes 3538944 | tf_op jit(solution)/shard_map/reduce_scatter | solution.py:12
  12.0 122.8 %copy-start.5 = (f32[256]{0:T(256)S(1)}, f32[256]{0:T(256)}, u32[]{:S(2)}) copy-start(f32[256]{0:T(256)} %param.8) | copy-start | bytes 3076
  12.0 169.2 %all-gather.4.cloned.1.call-start = ((), (), s32[]{:S(2)}) async-start(), calls=%async_computation.5 | async-start | bytes 1769472 | tf_op jit(solution)/shard_map/all_gather | solution.py:39
  89.6 45.2 %copy-start.3 = (f32[2048,48]{0,1:T(8,128)S(1)}, f32[2048,48]{0,1:T(8,128)}, u32[]{:S(2)}) copy-start(f32[2048,48]{0,1:T(8,128)} %reduce-scatter.5.cloned.1.call-done) | copy-start | bytes 1179652
  137.5 224.9 %copy-start.1 = (f32[2048,48]{0,1:T(8,128)}, f32[2048,48]{0,1:T(8,128)S(1)}, u32[]{:S(2)}) copy-start(f32[2048,48]{0,1:T(8,128)S(1)} %get-tuple-element.13) | copy-start | bytes 1179652
  137.6 137.4 %reduce-scatter.7.cloned.1.call-start = ((), (), s32[]{:S(2)}) async-start(), calls=%async_computation.6 | async-start | bytes 3538944 | tf_op jit(solution)/shard_map/reduce_scatter | solution.py:12
  200.2 0.7 copy-start.4
  200.3 208.4 %all-gather.6.cloned.1.call-start = ((), (), s32[]{:S(2)}) async-start(), calls=%async_computation.7 | async-start | bytes 1769472 | tf_op jit(solution)/shard_map/all_gather | solution.py:39
  364.4 138.0 %reduce-scatter.9.cloned.1.call-start = ((), (), s32[]{:S(2)}) async-start(), calls=%async_computation.8 | async-start | bytes 3538944 | tf_op jit(solution)/shard_map/reduce_scatter | solution.py:12
  427.7 206.7 %all-gather.8.cloned.1.call-start = ((), (), s32[]{:S(2)}) async-start(), calls=%async_computation.9 | async-start | bytes 1769472 | tf_op jit(solution)/shard_map/all_gather | solution.py:39
  590.1 138.1 %reduce-scatter.11.cloned.1.call-start = ((), (), s32[]{:S(2)}) async-start(), calls=%async_computation.10 | async-start | bytes 3538944 | tf_op jit(solution)/shard_map/reduce_scatter | solution.py:12
  653.4 74.8 %copy-start.2 = (f32[2048,48]{0,1:T(8,128)S(1)}, f32[2048,48]{0,1:T(8,128)}, u32[]{:S(2)}) copy-start(f32[2048,48]{0,1:T(8,128)} %copy-done.1) | copy-start | bytes 1179652
Sparse Core Ops, SparseCore 0:
  12.1 77.4 reduce-scatter.4
  137.7 43.4 all-gather.3
  200.4 74.5 reduce-scatter.6
  364.5 44.0 all-gather.5
  427.8 74.5 reduce-scatter.8
  590.2 44.1 all-gather.7
  653.6 74.6 reduce-scatter.10
where the time goes:
time: 739 us; the launch traced here: 737 us
  blocking collectives  355 us (48%)
  waiting for transfers between devices  308 us (42%)
  matrix products  49.8 us (7%)
  between operations  14.3 us (2%)
  other arithmetic  8.84 us (1%)
    reduce_scatter x4, waiting for transfers between devices, normal_terms(): lax.psum_scatter(lax.dot_general(design, rows_low, (((0,), (0,)), ((), ()...  176 us
    all_gather x3, waiting for transfers between devices, shards(): lax.all_gather(dir_low, 'row', axis=0, tiled=True)  132 us
    psum x3, blocking collectives, precondition(): projected = lax.psum(projected, ('row', 'feat'))  122 us
    psum x3, blocking collectives, precondition(): inner = lax.psum(jnp.sum(residual * search, axis=0), ('row', 'feat'))  120 us
    psum x2, blocking collectives, shards(): curvature = lax.psum(local_part, ('row', 'feat'))  82.4 us
    psum x3, blocking collectives, shards(): lax.psum(jnp.dot(design, lax.all_gather(dir_low, 'row', axis=0, tiled=Tru...  30.8 us
    dot_general x4, matrix products, normal_terms(): lax.dot_general(design, rows_low, (((0,), (0,)), ((), ())), preferred_ele...  18.3 us
  transfers between devices with their start and end apart: 7, of which 7 were waited for; matrix products, arithmetic and copies ran while one was open for 0% of the time, Pallas kernels for 0%

commit v1 on v0

v1 whole, which is shorter than its diff:
```python
import functools

import jax
import jax.numpy as jnp
from jax import lax
from jax.experimental import pallas as pl
from jax.experimental.pallas import tpu as pltpu
from jax.sharding import PartitionSpec as P

ITERS = 3
EXTRA = 16
LANES = 128
F32 = jnp.float32
BF16 = jnp.bfloat16
NT = (((1,), (1,)), ((), ()))


def to_column(row, count):
    return jnp.broadcast_to(row, (LANES, LANES)).T[:count, :1]


def kernel(
    n_row, n_feat, tile,
    design, targets, factor, weights, penalty, solution, residual,
    block, fbuf, ft, tall, direction, dlow,
    psend, precv, p2, p3, pfull,
    vsend, vrecv, v2, v3, vlow,
    load_sem, a_sem, t_sem, p1_sem, p2_sem, p3_sem, v1_sem, v2_sem, v3_sem,
):
    me = lax.axis_index("row")
    mf = lax.axis_index("feat")
    count, rows_dev = targets.shape
    width = block.shape[2]
    rows = n_row * rows_dev
    rank = ft.shape[0]
    part = rank // n_row
    tiles = width // tile
    pending = []

    def send(src, dst, sems, at_dest, at_src, axis, peer):
        copy = pltpu.make_async_remote_copy(
            src_ref=src,
            dst_ref=dst,
            send_sem=sems.at[0, *at_dest],
            recv_sem=sems.at[1, *at_src],
            device_id={axis: peer},
            device_id_type=pl.DeviceIdType.MESH,
        )
        copy.start()
        pending.append(copy)

    def arrived(dst, sems, at_src, axis, peer):
        pltpu.make_async_remote_copy(
            src_ref=dst,
            dst_ref=dst,
            send_sem=sems.at[0, *at_src],
            recv_sem=sems.at[1, *at_src],
            device_id={axis: peer},
            device_id_type=pl.DeviceIdType.MESH,
        ).wait_recv()

    def row_peers():
        return [lax.rem(me + off, n_row) for off in range(1, n_row)]

    def feat_peers():
        return [lax.rem(mf + off, n_feat) for off in range(1, n_feat)]

    load_f = pltpu.make_async_copy(factor, fbuf, load_sem.at[0])
    load_f.start()
    own = pltpu.make_async_copy(
        design.at[:, pl.ds(pl.multiple_of(me * width, width), width)], block.at[me], load_sem.at[1]
    )
    own.start()

    barrier = pltpu.get_barrier_semaphore()
    for peer in row_peers():
        pl.semaphore_signal(
            barrier, inc=1, device_id={"row": peer}, device_id_type=pl.DeviceIdType.MESH
        )
    for peer in feat_peers():
        pl.semaphore_signal(
            barrier, inc=1, device_id={"feat": peer}, device_id_type=pl.DeviceIdType.MESH
        )
    pl.semaphore_wait(barrier, n_row + n_feat - 2)

    my_rows = pl.ds(pl.multiple_of(me * rows_dev, rows_dev), rows_dev)
    for peer in row_peers():
        send(targets, tall.at[:, my_rows], t_sem, (peer,), (me,), "row", peer)
        send(
            design.at[:, pl.ds(pl.multiple_of(peer * width, width), width)],
            block.at[me], a_sem, (peer,), (me,), "row", peer,
        )

    psend[...] = jnp.zeros_like(psend)
    vsend[...] = jnp.zeros_like(vsend)
    for k in range(ITERS):
        p3[k] = jnp.zeros_like(p3[k])
    tall[:, my_rows] = targets[...]
    solution[...] = jnp.zeros_like(solution)
    load_f.wait()
    step_rows = min(width, 256)

    @pl.loop(0, width // step_rows)
    def _(j):
        at = pl.ds(pl.multiple_of(j * step_rows, step_rows), step_rows)
        ft[:, at] = fbuf[at, :].T.astype(BF16)

    own.wait()
    for peer in row_peers():
        arrived(tall.at[:, pl.ds(pl.multiple_of(peer * rows_dev, rows_dev), rows_dev)], t_sem, (peer,), "row", peer)
        arrived(block.at[peer], a_sem, (peer,), "row", peer)

    def times_block(low, at):
        return jnp.dot(low, block[:, :, at].reshape(rows, tile), preferred_element_type=F32)

    @pl.loop(0, tiles)
    def _(j):
        at = pl.ds(pl.multiple_of(j * tile, tile), tile)
        residual[:, at] = times_block(tall[...], at)

    def square_rows(value):
        low = (value * value).astype(BF16)
        sums = lax.dot_general(jnp.ones((EXTRA, width), BF16), low, NT, preferred_element_type=F32)
        at = lax.broadcasted_iota(jnp.int32, sums.shape, 0)
        high = sums.astype(BF16).astype(F32)
        return jnp.where(at == 0, high, jnp.where(at == 1, sums - high, 0.0))

    def row_total(k, sent, received, sems):
        total = sent[k, me].astype(F32)
        for peer in row_peers():
            arrived(received.at[k, peer], sems, (k, peer), "row", peer)
            total = total + received[k, peer].astype(F32)
        return total

    def feat_total(k, total, held, sems):
        held[k, mf] = total
        for peer in feat_peers():
            send(held.at[k, mf], held.at[k, mf], sems, (k, peer), (k, mf), "feat", peer)
        for peer in feat_peers():
            arrived(held.at[k, peer], sems, (k, peer), "feat", peer)
        total = held[k, 0]
        for index in range(1, n_feat):
            total = total + held[k, index]
        return total

    inner = None
    for k in range(ITERS):
        value = residual[...]
        projected = lax.dot_general(ft[...], value.astype(BF16), NT, preferred_element_type=F32)
        squares = square_rows(value).astype(psend.dtype)
        for index in range(n_row):
            psend[k, index, :part, :count] = projected[index * part : (index + 1) * part].astype(
                psend.dtype
            )
            psend[k, index, part:, :count] = squares
        for peer in row_peers():
            send(psend.at[k, peer], precv.at[k, me], p1_sem, (k, peer), (k, me), "row", peer)
        total = feat_total(k, row_total(k, psend, precv, p1_sem), p2, p2_sem)
        norm = jnp.sum(total[part:], axis=0, keepdims=True)
        p3[k] = total[:part].astype(p3.dtype)
        my_part = pl.ds(pl.multiple_of(me * part, part), part)
        pfull[k, my_part, :] = p3[k]
        for peer in row_peers():
            send(p3.at[k], pfull.at[k, my_part, :], p3_sem, (k, peer), (k, me), "row", peer)
        for peer in row_peers():
            arrived(
                pfull.at[k, pl.ds(pl.multiple_of(peer * part, part), part), :],
                p3_sem, (k, peer), "row", peer,
            )
        projected = pfull[k].astype(F32)
        weighted = weights[...] * projected
        inner_next = to_column(norm + jnp.sum(weighted * projected, axis=0, keepdims=True), count)
        weighted_low = weighted.T[:count].astype(BF16)
        ratio = None if inner is None else inner_next / inner
        inner = inner_next

        @pl.loop(0, tiles)
        def _(j):
            at = pl.ds(pl.multiple_of(j * tile, tile), tile)
            search = residual[:, at] + jnp.dot(
                weighted_low, ft[:, at], preferred_element_type=F32
            )
            if ratio is not None:
                search = search + ratio * direction[:, at]
            direction[:, at] = search
            dlow[:, at] = search.astype(BF16)

        squares = square_rows(direction[...]).astype(BF16)
        pairs = n_row // 2
        for off in list(range(1, pairs)) + [0]:
            pair = lax.rem(me // 2 + off, pairs)
            values = lax.dot_general(
                dlow[...],
                block[pl.ds(2 * pair, 2)].reshape(2 * rows_dev, width),
                NT,
                preferred_element_type=F32,
            ).astype(BF16)
            for half in range(2):
                vsend[k, 2 * pair + half, :count, :] = values[
                    :, half * rows_dev : (half + 1) * rows_dev
                ]
                vsend[k, 2 * pair + half, count:, :count] = squares
            if off:
                peers = [2 * pair, 2 * pair + 1]
            else:
                peers = [me + 1 - 2 * lax.rem(me, 2)]
            for peer in peers:
                send(vsend.at[k, peer], vrecv.at[k, me], v1_sem, (k, peer), (k, me), "row", peer)
        total = feat_total(k, row_total(k, vsend, vrecv, v1_sem), v2, v2_sem)
        norm = to_column(jnp.sum(total[count:], axis=0, keepdims=True), count)
        v3[k] = total[:count].astype(BF16)
        vlow[k, :, my_rows] = v3[k]
        for peer in row_peers():
            send(v3.at[k], vlow.at[k, :, my_rows], v3_sem, (k, peer), (k, me), "row", peer)
        for peer in row_peers():
            arrived(
                vlow.at[k, :, pl.ds(pl.multiple_of(peer * rows_dev, rows_dev), rows_dev)],
                v3_sem, (k, peer), "row", peer,
            )
        row_low = vlow[k]
        wide = row_low.astype(F32)
        curvature = jnp.sum(wide * wide, axis=1, keepdims=True) + penalty[...] * norm
        step = inner / curvature
        ridge = penalty[...]

        @pl.loop(0, tiles)
        def _(j):
            at = pl.ds(pl.multiple_of(j * tile, tile), tile)
            along = direction[:, at]
            solution[:, at] = solution[:, at] + step * along
            residual[:, at] = residual[:, at] - step * (times_block(row_low, at) + ridge * along)

    for copy in pending:
        copy.wait_send()


def shards(n_row, n_feat, design, targets, factor, weights, penalty):
    rows_dev, columns = design.shape
    width = columns // n_row
    count = targets.shape[1]
    rank = factor.shape[1]
    rows = n_row * rows_dev
    part = rank // n_row
    link = BF16 if part % 16 == 0 else F32
    vmem = pl.BlockSpec(memory_space=pltpu.VMEM)
    hbm = pl.BlockSpec(memory_space=pl.ANY)
    out = jax.ShapeDtypeStruct((count, width), F32)
    dma = pltpu.SemaphoreType.DMA
    solution, residual = pl.pallas_call(
        functools.partial(kernel, n_row, n_feat, min(width, 512)),
        out_shape=(out, out),
        in_specs=[hbm, vmem, hbm, vmem, vmem],
        out_specs=(vmem, vmem),
        scratch_shapes=[
            pltpu.VMEM((n_row, rows_dev, width), BF16),
            pltpu.VMEM((width, rank), F32),
            pltpu.VMEM((rank, width), BF16),
            pltpu.VMEM((count, rows), BF16),
            pltpu.VMEM((count, width), F32),
            pltpu.VMEM((count, width), BF16),
            pltpu.VMEM((ITERS, n_row, part + EXTRA, LANES), link),
            pltpu.VMEM((ITERS, n_row, part + EXTRA, LANES), link),
            pltpu.VMEM((ITERS, n_feat, part + EXTRA, LANES), F32),
            pltpu.VMEM((ITERS, part, LANES), link),
            pltpu.VMEM((ITERS, rank, LANES), link),
            pltpu.VMEM((ITERS, n_row, count + EXTRA, rows_dev), BF16),
            pltpu.VMEM((ITERS, n_row, count + EXTRA, rows_dev), BF16),
            pltpu.VMEM((ITERS, n_feat, count + EXTRA, rows_dev), F32),
            pltpu.VMEM((ITERS, count, rows_dev), BF16),
            pltpu.VMEM((ITERS, count, rows), BF16),
            dma((2,)),
            dma((2, n_row)),
            dma((2, n_row)),
            dma((2, ITERS, n_row)),
            dma((2, ITERS, n_feat)),
            dma((2, ITERS, n_row)),
            dma((2, ITERS, n_row)),
            dma((2, ITERS, n_feat)),
            dma((2, ITERS, n_row)),
        ],
        compiler_params=pltpu.CompilerParams(
            collective_id=0, has_side_effects=True, vmem_limit_bytes=40 * 1024 * 1024
        ),
    )(design, targets.T, factor, weights[:, None], penalty[:, None])
    return solution.T, residual.T


def solution(mesh):
    return jax.shard_map(
        functools.partial(shards, mesh.shape["row"], mesh.shape["feat"]),
        mesh=mesh,
        in_specs=(P("row", "feat"), P("row", None), P(("feat", "row"), None), P(), P()),
        out_specs=(P(("feat", "row"), None), P(("feat", "row"), None)),
        check_vma=False,
    )
```

time: 739 us -> 195 us (0.26)
  blocking collectives: 355 us -> 0 us
  waiting for transfers between devices: 308 us -> 0 us
  Pallas kernels: 0 us -> 187 us
  matrix products: 49.8 us -> 0 us
  between operations: 14.3 us -> 0.66 us
  other arithmetic: 8.84 us -> 0 us
    psum x11 -> x0, blocking collectives: 355 us -> none  [the longest x3 122 us: precondition(): projected = lax.psum(projected, ('row', 'feat'))]
    pallas_call x0 -> x1, Pallas kernels: none -> 187 us  [shards(): pl.pallas_call(functools.partial(kernel, n_row, n_feat, min(width, 512)),...]
    reduce_scatter x4 -> x0, waiting for transfers between devices: 176 us -> none  [normal_terms(): lax.psum_scatter(lax.dot_general(design, rows_low, (((0,), (0,)), ((), ()...]
    all_gather x3 -> x0, waiting for transfers between devices: 132 us -> none  [shards(): lax.all_gather(dir_low, 'row', axis=0, tiled=True)]
    dot_general x13 -> x0, matrix products: 49.8 us -> none  [the longest x4 18.3 us: normal_terms(): lax.dot_general(design, rows_low, (((0,), (0,)), ((), ())), preferred_ele...]
  transfers between devices with their start and end apart: 7 -> 0, of which waited for: 7 -> 0; matrix products, arithmetic and copies ran while one was open for 0% -> 0% of each run, Pallas kernels for 0% -> 0%
where the time goes in v1:
time: 195 us
  Pallas kernels  187 us (96%)
  local copies, waits for them, and re-layouts  7.52 us (4%)
    pallas_call x1, Pallas kernels, shards(): pl.pallas_call(functools.partial(kernel, n_row, n_feat, min(width, 512)),...  187 us
    unnamed x8, local copies, waits for them, and re-layouts  5.98 us

profile of v1, /device:TPU:0, one launch (start us, length us, event | category | flops | bytes accessed | tf_op | source)
XLA Modules:
  0.0 194.9 jit_solution(2610827952750665216)
XLA Ops:
  0.6 0.7 copy.9.penalty
  1.4 0.8 copy.8.weights
  2.2 0.0 copy-start
  2.2 2.2 %copy-done = bf16[128,16384]{1,0:T(8,128)(2,1)S(1)} copy-done((bf16[128,16384]{1,0:T(8,128)(2,1)S(1)}, bf16[128,16384]{1,0:T(8,128)(2,1)}, u32[]{:S(2)}) %copy-start) | copy-done | bytes 4194328
  4.4 0.0 copy-start.1
  4.4 1.6 copy-done.1
  6.0 0.0 copy-start.2
  6.0 0.7 copy-done.2
  6.7 186.7 %shard_map.68 = (f32[48,2048]{1,0:T(8,128)S(1)}, f32[48,2048]{1,0:T(8,128)S(1)}) custom-call(bf16[128,16384]{1,0:T(8,128)(2,1)S(1)} %copy-done, bf16[48,128]{1,0:T(8,128)(2,1)S(1)} %bitcast.7, f32[2048,256]{1,0:T(8,128)S(1)} %copy-done.1, f32[256,1]{1,0:T(8,128)S(1)} %copy.8.weights, f32[48,1]{1,0:T(8,128)S(1)} %copy.9.penalty), custom_call_target="tpu_custom_call" | custom-call | tf_op jit(solution)/shard_map/pallas_call | solution.py:249
  193.4 0.7 copy.12
  194.2 0.7 copy.13
Async XLA Ops:
  2.2 2.2 %copy-start = (bf16[128,16384]{1,0:T(8,128)(2,1)S(1)}, bf16[128,16384]{1,0:T(8,128)(2,1)}, u32[]{:S(2)}) copy-start(bf16[128,16384]{1,0:T(8,128)(2,1)} %design.1) | copy-start | bytes 12582916
  4.4 1.6 copy-start.1
  6.0 0.7 copy-start.2

commit v2 on v1

--- a/solution.py
+++ b/solution.py
@@ -22,14 +22,14 @@
 def kernel(
     n_row, n_feat, tile,
     design, targets, factor, weights, penalty, solution, residual,
-    block, fbuf, ft, tall, direction, dlow,
+    block, fbuf, ft, tlocal, wrow, prow, tall, direction, dlow,
     psend, precv, p2, p3, pfull,
     vsend, vrecv, v2, v3, vlow,
     load_sem, a_sem, t_sem, p1_sem, p2_sem, p3_sem, v1_sem, v2_sem, v3_sem,
 ):
     me = lax.axis_index("row")
     mf = lax.axis_index("feat")
-    count, rows_dev = targets.shape
+    count, rows_dev = tlocal.shape
     width = block.shape[2]
     rows = n_row * rows_dev
     rank = ft.shape[0]
@@ -65,6 +65,12 @@
     def feat_peers():
         return [lax.rem(mf + off, n_feat) for off in range(1, n_feat)]
 
+    load_t = pltpu.make_async_copy(targets, tlocal, load_sem.at[2])
+    load_t.start()
+    load_w = pltpu.make_async_copy(weights, wrow, load_sem.at[3])
+    load_w.start()
+    load_p = pltpu.make_async_copy(penalty, prow, load_sem.at[4])
+    load_p.start()
     load_f = pltpu.make_async_copy(factor, fbuf, load_sem.at[0])
     load_f.start()
     own = pltpu.make_async_copy(
@@ -84,8 +90,9 @@
     pl.semaphore_wait(barrier, n_row + n_feat - 2)
 
     my_rows = pl.ds(pl.multiple_of(me * rows_dev, rows_dev), rows_dev)
+    load_t.wait()
     for peer in row_peers():
-        send(targets, tall.at[:, my_rows], t_sem, (peer,), (me,), "row", peer)
+        send(tlocal, tall.at[:, my_rows], t_sem, (peer,), (me,), "row", peer)
         send(
             design.at[:, pl.ds(pl.multiple_of(peer * width, width), width)],
             block.at[me], a_sem, (peer,), (me,), "row", peer,
@@ -95,7 +102,7 @@
     vsend[...] = jnp.zeros_like(vsend)
     for k in range(ITERS):
         p3[k] = jnp.zeros_like(p3[k])
-    tall[:, my_rows] = targets[...]
+    tall[:, my_rows] = tlocal[...]
     solution[...] = jnp.zeros_like(solution)
     load_f.wait()
     step_rows = min(width, 256)
@@ -105,18 +112,30 @@
         at = pl.ds(pl.multiple_of(j * step_rows, step_rows), step_rows)
         ft[:, at] = fbuf[at, :].T.astype(BF16)
 
+    load_w.wait()
+    load_p.wait()
+    weight = jnp.broadcast_to(wrow[...], (LANES, rank)).T[:, :1]
+    ridge = jnp.broadcast_to(prow[...], (LANES, LANES)).T[:count, :1]
     own.wait()
-    for peer in row_peers():
+
+    def first_product(source, fresh):
+        low = tall[:, pl.ds(pl.multiple_of(source * rows_dev, rows_dev), rows_dev)]
+
+        @pl.loop(0, tiles)
+        def _(j):
+            at = pl.ds(pl.multiple_of(j * tile, tile), tile)
+            value = jnp.dot(low, block[source, :, at], preferred_element_type=F32)
+            residual[:, at] = value if fresh else residual[:, at] + value
+
+    first_product(me, True)
+    for off in range(1, n_row):
+        peer = lax.rem(me + n_row - off, n_row)
         arrived(tall.at[:, pl.ds(pl.multiple_of(peer * rows_dev, rows_dev), rows_dev)], t_sem, (peer,), "row", peer)
         arrived(block.at[peer], a_sem, (peer,), "row", peer)
+        first_product(peer, False)
 
     def times_block(low, at):
         return jnp.dot(low, block[:, :, at].reshape(rows, tile), preferred_element_type=F32)
-
-    @pl.loop(0, tiles)
-    def _(j):
-        at = pl.ds(pl.multiple_of(j * tile, tile), tile)
-        residual[:, at] = times_block(tall[...], at)
 
     def square_rows(value):
         low = (value * value).astype(BF16)
@@ -168,7 +187,7 @@
                 p3_sem, (k, peer), "row", peer,
             )
         projected = pfull[k].astype(F32)
-        weighted = weights[...] * projected
+        weighted = weight * projected
         inner_next = to_column(norm + jnp.sum(weighted * projected, axis=0, keepdims=True), count)
         weighted_low = weighted.T[:count].astype(BF16)
         ratio = None if inner is None else inner_next / inner
@@ -219,9 +238,8 @@
             )
         row_low = vlow[k]
         wide = row_low.astype(F32)
-        curvature = jnp.sum(wide * wide, axis=1, keepdims=True) + penalty[...] * norm
+        curvature = jnp.sum(wide * wide, axis=1, keepdims=True) + ridge * norm
         step = inner / curvature
-        ridge = penalty[...]
 
         @pl.loop(0, tiles)
         def _(j):
@@ -243,18 +261,21 @@
     part = rank // n_row
     link = BF16 if part % 16 == 0 else F32
     vmem = pl.BlockSpec(memory_space=pltpu.VMEM)
-    hbm = pl.BlockSpec(memory_space=pl.ANY)
+    hbm = pl.BlockSpec(memory_space=pltpu.HBM)
     out = jax.ShapeDtypeStruct((count, width), F32)
     dma = pltpu.SemaphoreType.DMA
     solution, residual = pl.pallas_call(
         functools.partial(kernel, n_row, n_feat, min(width, 512)),
         out_shape=(out, out),
-        in_specs=[hbm, vmem, hbm, vmem, vmem],
+        in_specs=[hbm] * 5,
         out_specs=(vmem, vmem),
         scratch_shapes=[
             pltpu.VMEM((n_row, rows_dev, width), BF16),
             pltpu.VMEM((width, rank), F32),
             pltpu.VMEM((rank, width), BF16),
+            pltpu.VMEM((count, rows_dev), BF16),
+            pltpu.VMEM((1, rank), F32),
+            pltpu.VMEM((1, LANES), F32),
             pltpu.VMEM((count, rows), BF16),
             pltpu.VMEM((count, width), F32),
             pltpu.VMEM((count, width), BF16),
@@ -268,7 +289,7 @@
             pltpu.VMEM((ITERS, n_feat, count + EXTRA, rows_dev), F32),
             pltpu.VMEM((ITERS, count, rows_dev), BF16),
             pltpu.VMEM((ITERS, count, rows), BF16),
-            dma((2,)),
+            dma((5,)),
             dma((2, n_row)),
             dma((2, n_row)),
             dma((2, ITERS, n_row)),
@@ -279,9 +300,9 @@
             dma((2, ITERS, n_row)),
         ],
         compiler_params=pltpu.CompilerParams(
-            collective_id=0, has_side_effects=True, vmem_limit_bytes=40 * 1024 * 1024
+            collective_id=0, has_side_effects=True, vmem_limit_bytes=65_000_000
         ),
-    )(design, targets.T, factor, weights[:, None], penalty[:, None])
+    )(design, targets.T, factor, weights[None, :], jnp.pad(penalty, (0, LANES - count))[None, :])
     return solution.T, residual.T
 
 

time: 195 us -> 194 us (level)
  local copies, waits for them, and re-layouts: 7.52 us -> 4.7 us
    unnamed x8 -> x2, local copies, waits for them, and re-layouts: 5.98 us -> 3.53 us
where the time goes in v2:
time: 194 us
  Pallas kernels  188 us (97%)
  local copies, waits for them, and re-layouts  4.7 us (2%)
    pallas_call x1, Pallas kernels, shards(): pl.pallas_call(functools.partial(kernel, n_row, n_feat, min(width, 512)),...  188 us

profile of v2, /device:TPU:0, one launch (start us, length us, event | category | flops | bytes accessed | tf_op | source)
XLA Modules:
  0.0 193.6 jit_solution(13555167791616147760)
XLA Ops:
  0.6 1.2 pad_bitcast_fusion.penalty
  1.8 188.3 %shard_map.68 = (f32[48,2048]{1,0:T(8,128)}, f32[48,2048]{1,0:T(8,128)}) custom-call(bf16[128,16384]{1,0:T(8,128)(2,1)} %design.1, bf16[48,128]{1,0:T(8,128)(2,1)} %bitcast.8, f32[2048,256]{1,0:T(8,128)} %factor.1, f32[1,256]{1,0:T(1,128)} %bitcast.9, f32[1,128]{1,0:T(1,128)} %pad_bitcast_fusion.penalty), custom_call_target="tpu_custom_call" | custom-call | tf_op jit(solution)/shard_map/pallas_call | solution.py:267
  190.1 1.8 copy.9
  191.9 1.8 copy.10

commit v3 on v2

--- a/solution.py
+++ b/solution.py
@@ -25,7 +25,10 @@
     block, fbuf, ft, tlocal, wrow, prow, tall, direction, dlow,
     psend, precv, p2, p3, pfull,
     vsend, vrecv, v2, v3, vlow,
+    kown, csend, crecv, cmid, crow, cfull,
+    msend, mrecv, m2, m3, mfull,
     load_sem, a_sem, t_sem, p1_sem, p2_sem, p3_sem, v1_sem, v2_sem, v3_sem,
+    ca_sem, cb_sem, cc_sem, cd_sem, m1_sem, m2_sem, m3_sem,
 ):
     me = lax.axis_index("row")
     mf = lax.axis_index("feat")
@@ -35,6 +38,7 @@
     rank = ft.shape[0]
     part = rank // n_row
     tiles = width // tile
+    piece = rows_dev // n_feat
     pending = []
 
     def send(src, dst, sems, at_dest, at_src, axis, peer):
@@ -100,8 +104,8 @@
 
     psend[...] = jnp.zeros_like(psend)
     vsend[...] = jnp.zeros_like(vsend)
-    for k in range(ITERS):
-        p3[k] = jnp.zeros_like(p3[k])
+    msend[...] = jnp.zeros_like(msend)
+    p3[...] = jnp.zeros_like(p3)
     tall[:, my_rows] = tlocal[...]
     solution[...] = jnp.zeros_like(solution)
     load_f.wait()
@@ -112,6 +116,7 @@
         at = pl.ds(pl.multiple_of(j * step_rows, step_rows), step_rows)
         ft[:, at] = fbuf[at, :].T.astype(BF16)
 
+    kown[...] = lax.dot_general(ft[...], ft[...], NT, preferred_element_type=F32)
     load_w.wait()
     load_p.wait()
     weight = jnp.broadcast_to(wrow[...], (LANES, rank)).T[:, :1]
@@ -127,22 +132,98 @@
             value = jnp.dot(low, block[source, :, at], preferred_element_type=F32)
             residual[:, at] = value if fresh else residual[:, at] + value
 
+    def cross_product(source):
+        cross = lax.dot_general(block[source], ft[...], NT, preferred_element_type=F32).astype(BF16)
+        for index in range(n_feat):
+            csend[source, index, :piece] = cross[index * piece : (index + 1) * piece]
+            at = lax.rem(source * n_feat + index, rank // EXTRA) * EXTRA
+            csend[source, index, piece:] = kown[pl.ds(pl.multiple_of(at, EXTRA), EXTRA), :].astype(
+                BF16
+            )
+        for peer in feat_peers():
+            send(
+                csend.at[source, peer], crecv.at[source, mf],
+                ca_sem, (source, peer), (source, mf), "feat", peer,
+            )
+
     first_product(me, True)
+    cross_product(me)
     for off in range(1, n_row):
         peer = lax.rem(me + n_row - off, n_row)
         arrived(tall.at[:, pl.ds(pl.multiple_of(peer * rows_dev, rows_dev), rows_dev)], t_sem, (peer,), "row", peer)
         arrived(block.at[peer], a_sem, (peer,), "row", peer)
         first_product(peer, False)
+        cross_product(peer)
 
     def times_block(low, at):
         return jnp.dot(low, block[:, :, at].reshape(rows, tile), preferred_element_type=F32)
 
-    def square_rows(value):
-        low = (value * value).astype(BF16)
+    def product_rows(left, right, first):
+        low = (left * right).astype(BF16)
         sums = lax.dot_general(jnp.ones((EXTRA, width), BF16), low, NT, preferred_element_type=F32)
         at = lax.broadcasted_iota(jnp.int32, sums.shape, 0)
         high = sums.astype(BF16).astype(F32)
-        return jnp.where(at == 0, high, jnp.where(at == 1, sums - high, 0.0))
+        return jnp.where(at == first, high, jnp.where(at == first + 1, sums - high, 0.0))
+
+    def square_rows(value):
+        return product_rows(value, value, 0)
+
+    def cross_to_rows():
+        for index in range(n_row):
+            for peer in feat_peers():
+                arrived(crecv.at[index, peer], ca_sem, (index, peer), "feat", peer)
+        for index in range(n_row):
+            total = csend[index, mf].astype(F32)
+            for off in range(1, n_feat):
+                total = total + crecv[index, lax.rem(mf + off, n_feat)].astype(F32)
+            cmid[index] = total.astype(BF16)
+        for peer in row_peers():
+            send(cmid.at[peer], crow.at[me], cb_sem, (peer,), (me,), "row", peer)
+
+    def cross_gather():
+        total = cmid[me].astype(F32)
+        for peer in row_peers():
+            arrived(crow.at[peer], cb_sem, (peer,), "row", peer)
+            total = total + crow[peer].astype(F32)
+        cfull[me, mf] = total.astype(BF16)
+        for peer in row_peers():
+            send(cfull.at[me, mf], cfull.at[me, mf], cc_sem, (peer,), (me,), "row", peer)
+
+    def cross_spread():
+        for peer in row_peers():
+            arrived(cfull.at[peer, mf], cc_sem, (peer,), "row", peer)
+        for peer in feat_peers():
+            send(cfull.at[:, mf], cfull.at[:, mf], cd_sem, (peer,), (mf,), "feat", peer)
+
+    def cross_finish():
+        for peer in feat_peers():
+            arrived(cfull.at[:, peer], cd_sem, (peer,), "feat", peer)
+        used = rank // EXTRA // n_feat
+        return (
+            cfull[:, :, :piece, :].reshape(rows, rank),
+            cfull[:used, :, piece:, :].reshape(rank, rank),
+        )
+
+    def send_products(k, low, sent, received, sems):
+        pairs = n_row // 2
+        for off in list(range(1, pairs)) + [0]:
+            pair = lax.rem(me // 2 + off, pairs)
+            values = lax.dot_general(
+                low,
+                block[pl.ds(2 * pair, 2)].reshape(2 * rows_dev, width),
+                NT,
+                preferred_element_type=F32,
+            ).astype(BF16)
+            for half in range(2):
+                sent[k, 2 * pair + half, :count, :] = values[
+                    :, half * rows_dev : (half + 1) * rows_dev
+                ]
+            if off:
+                peers = [2 * pair, 2 * pair + 1]
+            else:
+                peers = [me + 1 - 2 * lax.rem(me, 2)]
+            for peer in peers:
+                send(sent.at[k, peer], received.at[k, me], sems, (k, peer), (k, me), "row", peer)
 
     def row_total(k, sent, received, sems):
         total = sent[k, me].astype(F32)
@@ -162,8 +243,7 @@
             total = total + held[k, index]
         return total
 
-    inner = None
-    for k in range(ITERS):
+    for k in range(1):
         value = residual[...]
         projected = lax.dot_general(ft[...], value.astype(BF16), NT, preferred_element_type=F32)
         squares = square_rows(value).astype(psend.dtype)
@@ -174,6 +254,7 @@
             psend[k, index, part:, :count] = squares
         for peer in row_peers():
             send(psend.at[k, peer], precv.at[k, me], p1_sem, (k, peer), (k, me), "row", peer)
+        cross_to_rows()
         total = feat_total(k, row_total(k, psend, precv, p1_sem), p2, p2_sem)
         norm = jnp.sum(total[part:], axis=0, keepdims=True)
         p3[k] = total[:part].astype(p3.dtype)
@@ -188,10 +269,9 @@
             )
         projected = pfull[k].astype(F32)
         weighted = weight * projected
-        inner_next = to_column(norm + jnp.sum(weighted * projected, axis=0, keepdims=True), count)
+        inner_row = norm + jnp.sum(weighted * projected, axis=0, keepdims=True)
+        inner = to_column(inner_row, count)
         weighted_low = weighted.T[:count].astype(BF16)
-        ratio = None if inner is None else inner_next / inner
-        inner = inner_next
 
         @pl.loop(0, tiles)
         def _(j):
@@ -199,38 +279,22 @@
             search = residual[:, at] + jnp.dot(
                 weighted_low, ft[:, at], preferred_element_type=F32
             )
-            if ratio is not None:
-                search = search + ratio * direction[:, at]
             direction[:, at] = search
             dlow[:, at] = search.astype(BF16)
 
         squares = square_rows(direction[...]).astype(BF16)
-        pairs = n_row // 2
-        for off in list(range(1, pairs)) + [0]:
-            pair = lax.rem(me // 2 + off, pairs)
-            values = lax.dot_general(
-                dlow[...],
-                block[pl.ds(2 * pair, 2)].reshape(2 * rows_dev, width),
-                NT,
-                preferred_element_type=F32,
-            ).astype(BF16)
-            for half in range(2):
-                vsend[k, 2 * pair + half, :count, :] = values[
-                    :, half * rows_dev : (half + 1) * rows_dev
-                ]
-                vsend[k, 2 * pair + half, count:, :count] = squares
-            if off:
-                peers = [2 * pair, 2 * pair + 1]
-            else:
-                peers = [me + 1 - 2 * lax.rem(me, 2)]
-            for peer in peers:
-                send(vsend.at[k, peer], vrecv.at[k, me], v1_sem, (k, peer), (k, me), "row", peer)
+        for index in range(n_row):
+            vsend[k, index, count:, :count] = squares
+        send_products(k, dlow[...], vsend, vrecv, v1_sem)
+        cross_gather()
         total = feat_total(k, row_total(k, vsend, vrecv, v1_sem), v2, v2_sem)
-        norm = to_column(jnp.sum(total[count:], axis=0, keepdims=True), count)
+        norm_row = jnp.sum(total[count:], axis=0, keepdims=True)
+        norm = to_column(norm_row, count)
         v3[k] = total[:count].astype(BF16)
         vlow[k, :, my_rows] = v3[k]
         for peer in row_peers():
             send(v3.at[k], vlow.at[k, :, my_rows], v3_sem, (k, peer), (k, me), "row", peer)
+        cross_spread()
         for peer in row_peers():
             arrived(
                 vlow.at[k, :, pl.ds(pl.multiple_of(peer * rows_dev, rows_dev), rows_dev)],
@@ -247,6 +311,69 @@
             along = direction[:, at]
             solution[:, at] = solution[:, at] + step * along
             residual[:, at] = residual[:, at] - step * (times_block(row_low, at) + ridge * along)
+
+    low_cross = low_gram = None
+    previous = wide
+    for k in range(ITERS - 1):
+        value = residual[...]
+        dlow[...] = value.astype(BF16)
+        raw = lax.dot_general(ft[...], dlow[...], NT, preferred_element_type=F32).astype(BF16)
+        stats = (
+            product_rows(value, value, 0) + product_rows(direction[...], value, 2)
+        ).astype(BF16)
+        for index in range(n_row):
+            msend[k, index, count : count + part, :count] = raw[index * part : (index + 1) * part]
+            msend[k, index, count + part :, :count] = stats
+        send_products(k, dlow[...], msend, mrecv, m1_sem)
+        total = feat_total(k, row_total(k, msend, mrecv, m1_sem), m2, m2_sem)
+        m3[k] = total[: count + part].astype(BF16)
+        mfull[k, me] = m3[k]
+        for peer in row_peers():
+            send(m3.at[k], mfull.at[k, me], m3_sem, (k, peer), (k, me), "row", peer)
+        if low_cross is None:
+            low_cross, low_gram = cross_finish()
+            along_gram = jnp.dot(low_gram, weighted.astype(BF16), preferred_element_type=F32)
+            along = projected + along_gram
+        tail = total[count + part :]
+        at = lax.broadcasted_iota(jnp.int32, tail.shape, 0)
+        norm = jnp.sum(jnp.where(at < 2, tail, 0.0), axis=0, keepdims=True)
+        overlap = jnp.sum(jnp.where(at >= 2, tail, 0.0), axis=0, keepdims=True)
+        for peer in row_peers():
+            arrived(mfull.at[k, peer], m3_sem, (k, peer), "row", peer)
+        image = jnp.concatenate([mfull[k, q, :count, :] for q in range(n_row)], axis=1).astype(F32)
+        projected = jnp.concatenate(
+            [mfull[k, q, count:, :].astype(F32) for q in range(n_row)], axis=0
+        )
+        weighted = weight * projected
+        weighted_low = weighted.T[:count].astype(BF16)
+        gain = jnp.sum(weighted * projected, axis=0, keepdims=True)
+        ratio_row = (norm + gain) / inner_row
+        inner_row = norm + gain
+        inner = to_column(inner_row, count)
+        ratio = to_column(ratio_row, count)
+        image = image + lax.dot_general(weighted_low, low_cross, NT, preferred_element_type=F32)
+        image = image + ratio * previous
+        row_low = image.astype(BF16)
+        wide = row_low.astype(F32)
+        previous = image
+        along_gram = jnp.dot(low_gram, weighted.astype(BF16), preferred_element_type=F32)
+        squared = norm + 2.0 * gain + jnp.sum(weighted * along_gram, axis=0, keepdims=True)
+        mixed = overlap + jnp.sum(along * weighted, axis=0, keepdims=True)
+        norm_row = squared + 2.0 * ratio_row * mixed + ratio_row * ratio_row * norm_row
+        along = projected + along_gram + ratio_row * along
+        curvature = jnp.sum(wide * wide, axis=1, keepdims=True) + ridge * to_column(norm_row, count)
+        step = inner / curvature
+
+        @pl.loop(0, tiles)
+        def _(j):
+            at = pl.ds(pl.multiple_of(j * tile, tile), tile)
+            search = residual[:, at] + jnp.dot(
+                weighted_low, ft[:, at], preferred_element_type=F32
+            )
+            search = search + ratio * direction[:, at]
+            direction[:, at] = search
+            solution[:, at] = solution[:, at] + step * search
+            residual[:, at] = residual[:, at] - step * (times_block(row_low, at) + ridge * search)
 
     for copy in pending:
         copy.wait_send()
@@ -259,6 +386,8 @@
     rank = factor.shape[1]
     rows = n_row * rows_dev
     part = rank // n_row
+    piece = rows_dev // n_feat + EXTRA
+    merged = count + part + EXTRA
     link = BF16 if part % 16 == 0 else F32
     vmem = pl.BlockSpec(memory_space=pltpu.VMEM)
     hbm = pl.BlockSpec(memory_space=pltpu.HBM)
@@ -279,25 +408,43 @@
             pltpu.VMEM((count, rows), BF16),
             pltpu.VMEM((count, width), F32),
             pltpu.VMEM((count, width), BF16),
-            pltpu.VMEM((ITERS, n_row, part + EXTRA, LANES), link),
-            pltpu.VMEM((ITERS, n_row, part + EXTRA, LANES), link),
-            pltpu.VMEM((ITERS, n_feat, part + EXTRA, LANES), F32),
-            pltpu.VMEM((ITERS, part, LANES), link),
-            pltpu.VMEM((ITERS, rank, LANES), link),
-            pltpu.VMEM((ITERS, n_row, count + EXTRA, rows_dev), BF16),
-            pltpu.VMEM((ITERS, n_row, count + EXTRA, rows_dev), BF16),
-            pltpu.VMEM((ITERS, n_feat, count + EXTRA, rows_dev), F32),
-            pltpu.VMEM((ITERS, count, rows_dev), BF16),
-            pltpu.VMEM((ITERS, count, rows), BF16),
+            pltpu.VMEM((1, n_row, part + EXTRA, LANES), link),
+            pltpu.VMEM((1, n_row, part + EXTRA, LANES), link),
+            pltpu.VMEM((1, n_feat, part + EXTRA, LANES), F32),
+            pltpu.VMEM((1, part, LANES), link),
+            pltpu.VMEM((1, rank, LANES), link),
+            pltpu.VMEM((1, n_row, count + EXTRA, rows_dev), BF16),
+            pltpu.VMEM((1, n_row, count + EXTRA, rows_dev), BF16),
+            pltpu.VMEM((1, n_feat, count + EXTRA, rows_dev), F32),
+            pltpu.VMEM((1, count, rows_dev), BF16),
+            pltpu.VMEM((1, count, rows), BF16),
+            pltpu.VMEM((rank, rank), F32),
+            pltpu.VMEM((n_row, n_feat, piece, rank), BF16),
+            pltpu.VMEM((n_row, n_feat, piece, rank), BF16),
+            pltpu.VMEM((n_row, piece, rank), BF16),
+            pltpu.VMEM((n_row, piece, rank), BF16),
+            pltpu.VMEM((n_row, n_feat, piece, rank), BF16),
+            pltpu.VMEM((ITERS - 1, n_row, merged, rows_dev), BF16),
+            pltpu.VMEM((ITERS - 1, n_row, merged, rows_dev), BF16),
+            pltpu.VMEM((ITERS - 1, n_feat, merged, rows_dev), F32),
+            pltpu.VMEM((ITERS - 1, count + part, rows_dev), BF16),
+            pltpu.VMEM((ITERS - 1, n_row, count + part, rows_dev), BF16),
             dma((5,)),
             dma((2, n_row)),
             dma((2, n_row)),
-            dma((2, ITERS, n_row)),
-            dma((2, ITERS, n_feat)),
-            dma((2, ITERS, n_row)),
-            dma((2, ITERS, n_row)),
-            dma((2, ITERS, n_feat)),
-            dma((2, ITERS, n_row)),
+            dma((2, 1, n_row)),
+            dma((2, 1, n_feat)),
+            dma((2, 1, n_row)),
+            dma((2, 1, n_row)),
+            dma((2, 1, n_feat)),
+            dma((2, 1, n_row)),
+            dma((2, n_row, n_feat)),
+            dma((2, n_row)),
+            dma((2, n_row)),
+            dma((2, n_feat)),
+            dma((2, ITERS - 1, n_row)),
+            dma((2, ITERS - 1, n_feat)),
+            dma((2, ITERS - 1, n_row)),
         ],
         compiler_params=pltpu.CompilerParams(
             collective_id=0, has_side_effects=True, vmem_limit_bytes=65_000_000

time: 194 us -> 181 us (0.933)
  Pallas kernels: 188 us -> 175 us
    pallas_call x1, Pallas kernels: 188 us -> 175 us  [shards(): pl.pallas_call(functools.partial(kernel, n_row, n_feat, min(width, 512)),...]
where the time goes in v3:
time: 181 us
  Pallas kernels  175 us (97%)
  local copies, waits for them, and re-layouts  4.7 us (3%)
    pallas_call x1, Pallas kernels, shards(): pl.pallas_call(functools.partial(kernel, n_row, n_feat, min(width, 512)),...  175 us

profile of v3, /device:TPU:0, one launch (start us, length us, event | category | flops | bytes accessed | tf_op | source)
XLA Modules:
  0.0 180.7 jit_solution(3874035726827034553)
XLA Ops:
  0.6 1.2 pad_bitcast_fusion.penalty
  1.8 175.3 %shard_map.68 = (f32[48,2048]{1,0:T(8,128)}, f32[48,2048]{1,0:T(8,128)}) custom-call(bf16[128,16384]{1,0:T(8,128)(2,1)} %design.1, bf16[48,128]{1,0:T(8,128)(2,1)} %bitcast.8, f32[2048,256]{1,0:T(8,128)} %factor.1, f32[1,256]{1,0:T(1,128)} %bitcast.9, f32[1,128]{1,0:T(1,128)} %pad_bitcast_fusion.penalty), custom_call_target="tpu_custom_call" | custom-call | tf_op jit(solution)/shard_map/pallas_call | solution.py:396
  177.1 1.8 copy.9
  178.9 1.8 copy.10
